TPU v7x, 512 devices: a whole 4x4x16 slice. The times are simulated.
512 devices in a mesh: dp: 16 (over z), pipe: 4 (over x), tensor: 8 (over y, core).
Axes of the slice: x: 4, y: 4, z: 16, core: 2. Of those that a mesh axis runs over, the one named last changes fastest.
Arguments:
- tokens: bfloat16 [16384, 8192], P('dp', ('pipe', 'tensor')), may hold values from -6 to 6
- key_value_weight: bfloat16 [8192, 2048], P(('pipe', 'tensor')), may hold values from -0.0625 to 0.0625
- adapter_down: bfloat16 [96, 8192, 128], P(None, ('pipe', 'tensor', 'dp')), may hold values from -0.0625 to 0.0625
- adapter_up: bfloat16 [96, 64, 2048], P(None, 'dp'), may hold values from -0.75 to 0.75
- tenant_of_block: int32 [128], replicated, may hold values from 0 to 95
- slot_of_tenant: int32 [96], replicated, may hold values from 0 to 95, each once
- cotangent: bfloat16 [16384, 2048], P(('dp', 'pipe', 'tensor')), may hold values from -1.5 to 1.5
Outputs:
- key_value: bfloat16 [16384, 2048], P(('dp', 'pipe', 'tensor'))
- input_grad: bfloat16 [16384, 8192], P('dp', ('pipe', 'tensor'))
- grad_a: float32 [96, 8192, 128], P(None, ('pipe', 'tensor', 'dp'))
- grad_b: float32 [96, 64, 2048], P(None, 'dp', ('pipe', 'tensor'))
Inputs may be any that keep to these rules, and one draw needn't show every extreme that they name: `slot_of_tenant`: each slot holds exactly one tenant.
All inputs are finite; a program needn't handle non-finite values.
Results may differ from a plain program's by a relative error of at most 0.017.
Values may be sent and summed in bfloat16 or wider, within the bound.
A program may use at most 64 MiB of HBM per device.

v0:
```python
import jax
import jax.numpy as jnp
from jax import lax
from jax.sharding import PartitionSpec as P

KEY_WIDTH = 1024
ADAPTER_RANK = 64
BLOCK = 128


def body(
    tokens, key_value_weight, adapter_down, adapter_up, tenant_of_block, slot_of_tenant, cotangent
):
    data_count = lax.axis_size("dp")
    group_count = lax.axis_size(("pipe", "tensor"))
    my_group = lax.axis_index(("pipe", "tensor"))
    tok_dev, feature_count = tokens.shape
    blocks_dev = tok_dev // BLOCK
    row_count = tok_dev // group_count
    tenant_list = slot_of_tenant.shape[0]
    all_blocks = tenant_of_block.shape[0]
    tenant_ids = lax.broadcasted_iota(jnp.int32, (all_blocks, tenant_list), 1)
    slot_of_block = jnp.sum(
        jnp.where(tenant_of_block[:, None] == tenant_ids, slot_of_tenant[None, :], 0), axis=1
    )
    slot_match = slot_of_block[:, None] == tenant_ids
    down_rows = adapter_down.shape[1]
    a_send = jnp.dot(
        slot_match.astype(jnp.bfloat16),
        adapter_down.reshape(tenant_list, down_rows * 2 * ADAPTER_RANK),
        preferred_element_type=jnp.float32,
    )
    a_send = a_send.astype(jnp.bfloat16).reshape(all_blocks, down_rows, 2 * ADAPTER_RANK)
    own_block = my_group * row_count // BLOCK
    own_slots = lax.dynamic_index_in_dim(
        slot_of_block.reshape(data_count, blocks_dev), own_block, 1, False
    )
    owner_choice = (
        own_slots[:, None] == lax.broadcasted_iota(jnp.int32, (data_count, tenant_list), 1)
    ).astype(jnp.bfloat16)
    up_rows = adapter_up.shape[1]
    b_send = jnp.dot(
        owner_choice,
        adapter_up.reshape(tenant_list, up_rows * 2 * KEY_WIDTH),
        preferred_element_type=jnp.float32,
    )
    b_send = b_send.astype(jnp.bfloat16).reshape(data_count, up_rows, 2 * KEY_WIDTH)
    down_blocks, b_own = (
        lax.all_to_all(a_send, "dp", split_axis=0, concat_axis=1, tiled=True),
        lax.all_to_all(b_send, "dp", split_axis=0, concat_axis=1, tiled=True),
    )
    b_own = b_own[0]
    tok_blocks = tokens.reshape(blocks_dev, BLOCK, feature_count)
    low_part = jnp.einsum(
        "bif,bfr->bir", tok_blocks, down_blocks, preferred_element_type=jnp.float32
    ).reshape(tok_dev, 2 * ADAPTER_RANK)
    low_all = lax.psum(low_part.astype(jnp.bfloat16), ("pipe", "tensor"))
    base_out = lax.psum_scatter(
        jnp.dot(tokens, key_value_weight, preferred_element_type=jnp.float32).astype(jnp.bfloat16),
        ("pipe", "tensor"),
        scatter_dimension=0,
        tiled=True,
    ).astype(jnp.float32)
    low_rows = lax.dynamic_slice_in_dim(low_all, my_group * row_count, row_count, 0)
    lowrank = jnp.concatenate(
        [
            jnp.dot(
                low_rows[:, :ADAPTER_RANK], b_own[:, :KEY_WIDTH], preferred_element_type=jnp.float32
            ),
            jnp.dot(
                low_rows[:, ADAPTER_RANK:], b_own[:, KEY_WIDTH:], preferred_element_type=jnp.float32
            ),
        ],
        axis=1,
    )
    key_value = (base_out + lowrank).astype(jnp.bfloat16)
    contract_last = (((1,), (1,)), ((), ()))
    grad_rows = jnp.concatenate(
        [
            lax.dot_general(
                cotangent[:, :KEY_WIDTH],
                b_own[:, :KEY_WIDTH],
                contract_last,
                preferred_element_type=jnp.float32,
            ),
            lax.dot_general(
                cotangent[:, KEY_WIDTH:],
                b_own[:, KEY_WIDTH:],
                contract_last,
                preferred_element_type=jnp.float32,
            ),
        ],
        axis=1,
    )
    grad_rows = grad_rows.astype(jnp.bfloat16)
    cot_all, grad_low = (
        lax.all_gather(cotangent, ("pipe", "tensor"), axis=0, tiled=True),
        lax.all_gather(grad_rows, ("pipe", "tensor"), axis=0, tiled=True),
    )
    grad_blocks = grad_low.reshape(blocks_dev, BLOCK, 2 * ADAPTER_RANK)
    input_grad = lax.dot_general(
        cot_all, key_value_weight, contract_last, preferred_element_type=jnp.float32
    )
    input_grad = input_grad + jnp.einsum(
        "bir,bfr->bif", grad_blocks, down_blocks, preferred_element_type=jnp.float32
    ).reshape(tok_dev, feature_count)
    input_grad = input_grad.astype(jnp.bfloat16)
    grad_a_part = jnp.einsum(
        "bif,bir->bfr", tok_blocks, grad_blocks, preferred_element_type=jnp.float32
    )
    col_count = 2 * KEY_WIDTH // group_count
    col_start = my_group * col_count
    half_index = col_start // KEY_WIDTH
    low_half = lax.dynamic_slice_in_dim(
        low_all, half_index * ADAPTER_RANK, ADAPTER_RANK, 1
    ).reshape(blocks_dev, BLOCK, ADAPTER_RANK)
    cot_cols = lax.dynamic_slice_in_dim(cot_all, col_start, col_count, 1).reshape(
        blocks_dev, BLOCK, col_count
    )
    grad_b_part = jnp.einsum("bir,bic->brc", low_half, cot_cols, preferred_element_type=jnp.float32)
    grad_a_recv, grad_b_recv = (
        lax.all_to_all(
            grad_a_part.astype(jnp.bfloat16), "dp", split_axis=1, concat_axis=0, tiled=True
        ).astype(grad_a_part.dtype),
        lax.all_to_all(
            grad_b_part.astype(jnp.bfloat16), "dp", split_axis=1, concat_axis=0, tiled=True
        ).astype(grad_b_part.dtype),
    )
    slot_weight = slot_match.astype(jnp.float32)
    grad_a = jnp.einsum(
        "bt,bx->tx",
        slot_weight,
        grad_a_recv.reshape(all_blocks, down_rows * 2 * ADAPTER_RANK),
        precision=lax.Precision.HIGHEST,
    )
    grad_a = grad_a.reshape(tenant_list, down_rows, 2 * ADAPTER_RANK)
    grad_b = jnp.einsum(
        "bt,bx->tx",
        slot_weight,
        grad_b_recv.reshape(all_blocks, grad_b_recv.shape[1] * col_count),
        precision=lax.Precision.HIGHEST,
    )
    grad_b = grad_b.reshape(tenant_list, grad_b_recv.shape[1], col_count)
    return (key_value, input_grad, grad_a, grad_b)


def solution(mesh):
    placed = (
        P("dp", ("pipe", "tensor")),
        P(("pipe", "tensor"), None),
        P(None, ("pipe", "tensor", "dp"), None),
        P(None, "dp", None),
        P(),
        P(),
        P(("dp", "pipe", "tensor"), None),
    )
    return jax.shard_map(
        body,
        mesh=mesh,
        in_specs=placed,
        out_specs=(
            P(("dp", "pipe", "tensor"), None),
            P("dp", ("pipe", "tensor")),
            P(None, ("pipe", "tensor", "dp"), None),
            P(None, "dp", ("pipe", "tensor")),
        ),
        check_vma=False,
    )
```

profile of v0, /device:TPU:1, one launch (start us, length us, event | category | flops | bytes accessed | tf_op | source)
XLA Modules:
  0.0 394.8 jit_solution(17106891758424243477)
XLA Ops:
  7.2 0.9 select_reduce_fusion
  8.1 1.3 fusion.2
  9.6 38.5 %all_to_all.57 = bf16[128,16,128]{2,1,0:T(8,128)(2,1)S(1)} all-to-all(bf16[128,16,128]{2,1,0:T(8,128)(2,1)S(1)} %bitcast.78), channel_id=1, replica_groups=mesh['dp'=16,'pipe'=4,'tensor'=8] {'dp'}, dimensions={0} | all-to-all | bytes 1048576 | tf_op jit(solution)/shard_map/all_to_all | solution.py:49
  48.2 0.8 copy-done.2
  49.0 0.3 convolution_convert_fusion.4
  49.3 0.9 copy.41
  50.2 3.2 convolution_convert_fusion.1
  53.5 0.7 all-gather.2.cloned.1.call-update
  54.3 2.4 copy.61
  56.9 0.4 convolution_convert_fusion
  57.5 26.0 %all_to_all.58 = bf16[16,4,2048]{2,1,0:T(4,128)(2,1)S(1)} all-to-all(bf16[16,4,2048]{2,1,0:T(4,128)(2,1)S(1)} %reshape.64), channel_id=1, replica_groups=mesh['dp'=16,'pipe'=4,'tensor'=8] {'dp'}, dimensions={0} | all-to-all | bytes 524288 | tf_op jit(solution)/shard_map/all_to_all | solution.py:50
  83.9 0.4 copy-done.4
  84.4 30.5 %all_gather.7 = bf16[1024,128]{1,0:T(8,128)(2,1)S(1)} all-gather(bf16[32,128]{1,0:T(8,128)(2,1)S(1)} %pad_maximum_fusion), channel_id=1, replica_groups=mesh['dp'=16,'pipe'=4,'tensor'=8] {'pipe','tensor'}, dimensions={0}, use_global_device_ids=true | all-gather | bytes 270336 | tf_op jit(solution)/shard_map/all_gather | solution.py:98
  114.9 0.3 fusion.1
  115.2 1.1 copy.43
  116.3 5.5 %all-to-all-start.2 = ((bf16[8,256,128]{2,0,1:T(8,128)(2,1)}), bf16[8,256,128]{2,0,1:T(8,128)(2,1)S(1)}, u32[]{:S(2)}, u32[]{:S(2)}) async-start(bf16[8,256,128]{2,0,1:T(8,128)(2,1)} %copy.43), calls=%async_computation.3 | async-start | bytes 1048576 | tf_op jit(solution)/shard_map/all_to_all | solution.py:122
  121.9 0.3 fusion.30
  122.2 63.9 %all-reduce.2.cloned.1.call-done = bf16[1024,128]{0,1:T(8,128)(2,1)} async-done(((bf16[1024,128]{0,1:T(8,128)(2,1)}), bf16[1024,128]{0,1:T(8,128)(2,1)}) %all-reduce.2.cloned.1.call-update) | async-done | bytes 262160 | tf_op jit(solution)/shard_map/psum | solution.py:57
  186.1 1.2 fusion.14
  187.3 1.2 fusion.11
  188.7 0.3 fusion.21
  189.1 1.3 copy.53
  190.4 103.8 %reduce-scatter.2.cloned.1.call-done = bf16[32,2048]{1,0:T(8,128)(2,1)} async-done(((bf16[1024,2048]{1,0:T(8,128)(2,1)}), bf16[32,2048]{1,0:T(8,128)(2,1)}) %reduce-scatter.2.cloned.1.call-update) | async-done | bytes 131088 | tf_op jit(solution)/shard_map/reduce_scatter | solution.py:58
  294.2 1.6 fusion.7
  295.8 64.5 %all-gather.2.cloned.1.call-done = bf16[1024,2048]{1,0:T(8,128)(2,1)} async-done(((bf16[32,2048]{1,0:T(8,128)(2,1)}), bf16[1024,2048]{1,0:T(8,128)(2,1)}) %all-gather.2.cloned.1.call-update) | async-done | bytes 4194320 | tf_op jit(solution)/shard_map/all_gather | solution.py:97
  360.3 1.1 constant_dynamic-slice_fusion
  361.4 1.1 convolution_convert_fusion.5
  362.6 0.8 reshape.73
  363.4 12.0 %all-to-all-start.3 = ((bf16[16,2,1024]{2,1,0:T(2,128)(2,1)}), bf16[16,2,1024]{2,1,0:T(2,128)(2,1)S(1)}, u32[]{:S(2)}, u32[]{:S(2)}) async-start(bf16[16,2,1024]{2,1,0:T(2,128)(2,1)} %reshape.73), calls=%async_computation.4 | async-start | bytes 131072 | tf_op jit(solution)/shard_map/all_to_all | solution.py:125
  375.4 4.3 %fusion = bf16[1024,256]{1,0:T(8,128)(2,1)} fusion(f32[1024,256]{1,0:T(8,128)S(1)} %bitcast.81, bf16[1024,2048]{1,0:T(8,128)(2,1)} %all-gather.2.cloned.1.call-done, bf16[256,2048]{1,0:T(8,128)(2,1)S(1)} %copy-done), kind=kOutput, calls=%fused_computation.4 | convolution fusion | flops 1074266112 | bytes 6815744 | tf_op jit(solution)/shard_map/dot_general | solution.py:101
  379.7 7.3 %all-to-all-done.3 = bf16[16,2,1024]{2,1,0:T(2,128)(2,1)S(1)} async-done(((bf16[16,2,1024]{2,1,0:T(2,128)(2,1)}), bf16[16,2,1024]{2,1,0:T(2,128)(2,1)S(1)}, u32[]{:S(2)}, u32[]{:S(2)}) %all-to-all-start.3) | async-done | bytes 65568 | tf_op jit(solution)/shard_map/all_to_all | solution.py:125
  387.5 0.8 fusion.19
  (31 shorter events, 2.0 us)
Async XLA Ops:
  7.2 43.0 %copy-start = (bf16[256,2048]{1,0:T(8,128)(2,1)S(1)}, bf16[256,2048]{1,0:T(8,128)(2,1)}, u32[]{:S(2)}) copy-start(bf16[256,2048]{1,0:T(8,128)(2,1)} %param.8) | copy-start | bytes 3145732
  7.2 41.8 %copy-start.1 = (bf16[1024,256]{1,0:T(8,128)(2,1)S(1)}, bf16[1024,256]{1,0:T(8,128)(2,1)}, u32[]{:S(2)}) copy-start(bf16[1024,256]{1,0:T(8,128)(2,1)} %param.7) | copy-start | bytes 1572868
  7.2 178.9 %all-reduce.2.cloned.1.call-start = ((), (), s32[]{:S(2)}) async-start(), calls=%async_computation.6 | async-start | bytes 524288 | tf_op jit(solution)/shard_map/psum | solution.py:57
  48.2 0.8 copy-start.2
  50.1 244.1 %reduce-scatter.2.cloned.1.call-start = ((), (), s32[]{:S(2)}) async-start(), calls=%async_computation.5 | async-start | bytes 4325376 | tf_op jit(solution)/shard_map/reduce_scatter | solution.py:58
  53.5 30.1 %copy-start.5 = (bf16[32,2048]{1,0:T(8,128)(2,1)S(1)}, bf16[32,2048]{1,0:T(8,128)(2,1)}, u32[]{:S(2)}) copy-start(bf16[32,2048]{1,0:T(8,128)(2,1)} %param.13) | copy-start | bytes 393220
  53.5 306.8 %all-gather.2.cloned.1.call-start = ((), (), s32[]{:S(2)}) async-start(), calls=%async_computation.7 | async-start | bytes 4325376 | tf_op jit(solution)/shard_map/all_gather | solution.py:97
  57.3 64.6 %copy-start.3 = (bf16[16,8,16,128]{3,2,0,1:T(8,128)(2,1)S(1)}, bf16[16,8,16,128]{3,2,0,1:T(8,128)(2,1)}, u32[]{:S(2)}) copy-start(bf16[16,8,16,128]{3,2,0,1:T(8,128)(2,1)} %copy-done.2) | copy-start | bytes 1572868
  83.6 0.7 copy-start.4
  116.3 72.1 %all-to-all-start.2 = ((bf16[8,256,128]{2,0,1:T(8,128)(2,1)}), bf16[8,256,128]{2,0,1:T(8,128)(2,1)S(1)}, u32[]{:S(2)}, u32[]{:S(2)}) async-start(bf16[8,256,128]{2,0,1:T(8,128)(2,1)} %copy.43), calls=%async_computation.3 | async-start | bytes 1048576 | tf_op jit(solution)/shard_map/all_to_all | solution.py:122
  363.4 23.6 %all-to-all-start.3 = ((bf16[16,2,1024]{2,1,0:T(2,128)(2,1)}), bf16[16,2,1024]{2,1,0:T(2,128)(2,1)S(1)}, u32[]{:S(2)}, u32[]{:S(2)}) async-start(bf16[16,2,1024]{2,1,0:T(2,128)(2,1)} %reshape.73), calls=%async_computation.4 | async-start | bytes 131072 | tf_op jit(solution)/shard_map/all_to_all | solution.py:125
Sparse Core Ops, SparseCore 0:
  50.3 135.7 all-reduce.1
  190.6 103.5 reduce-scatter.1
  297.4 62.9 all-gather.1
where the time goes:
time: 396 us; the launch traced here: 395 us
  waiting for transfers between devices  240 us (61%)
  blocking collectives  95 us (24%)
  starting transfers between devices  17.7 us (4%)
  matrix products  15.1 us (4%)
  between operations  14 us (4%)
  local copies, waits for them, and re-layouts  10.2 us (3%)
    reduce_scatter x1, waiting for transfers between devices, body(): lax.psum_scatter(jnp.dot(tokens, key_value_weight, preferred_element_type...  104 us
    all_gather x1, waiting for transfers between devices, body(): lax.all_gather(cotangent, ('pipe', 'tensor'), axis=0, tiled=True)  64.5 us
    psum x1, waiting for transfers between devices, body(): low_all = lax.psum(low_part.astype(jnp.bfloat16), ('pipe', 'tensor'))  63.9 us
    all_to_all x1, blocking collectives, body(): lax.all_to_all(a_send, 'dp', split_axis=0, concat_axis=1, tiled=True)  38.5 us
    all_gather x1, blocking collectives, body(): lax.all_gather(grad_rows, ('pipe', 'tensor'), axis=0, tiled=True)  30.5 us
    all_to_all x1, blocking collectives, body(): lax.all_to_all(b_send, 'dp', split_axis=0, concat_axis=1, tiled=True)  26 us
    all_to_all x1, starting transfers between devices, body(): lax.all_to_all(grad_b_part.astype(jnp.bfloat16), 'dp', split_axis=1, conc...  12 us
  transfers between devices with their start and end apart: 5, of which 4 were waited for; matrix products, arithmetic and copies ran while one was open for 5% of the time, Pallas kernels for 0%

commit v1 on v0

v1 whole, which is shorter than its diff:
```python
import functools

import jax
import jax.numpy as jnp
from jax import lax
from jax.experimental import pallas as pl
from jax.experimental.pallas import tpu as pltpu
from jax.sharding import PartitionSpec as P

MESH = pl.DeviceIdType.MESH
F32, BF16, I32 = jnp.float32, jnp.bfloat16, jnp.int32
NZ, NX, NY = 16, 4, 4
SLOTS, UP, DOWN, RANKS = 96, 4, 16, 128
BLOCKS = 8
ROWS, FEATS, WIDTH, HALF, QUARTER = 32, 256, 2048, 1024, 512
COLS = 64


def scratches():
    return dict(
        au=pltpu.VMEM((SLOTS, UP, WIDTH), BF16),
        ad=pltpu.VMEM((SLOTS, DOWN, RANKS), BF16),
        xv=pltpu.VMEM((NX, NY, 2, ROWS, FEATS), BF16),
        wv=pltpu.VMEM((FEATS, WIDTH), BF16),
        xp=pltpu.VMEM((NX, NY, ROWS, FEATS), BF16),
        wp=pltpu.VMEM((FEATS, WIDTH), BF16),
        bsend=pltpu.VMEM((NZ, UP, QUARTER), BF16),
        brecv=pltpu.VMEM((NZ, UP, QUARTER), BF16),
        bqf=pltpu.VMEM((NZ * UP, QUARTER), F32),
        bown=pltpu.VMEM((4, NZ * UP, QUARTER), BF16),
        asend=pltpu.VMEM((NZ, BLOCKS, DOWN, RANKS), BF16),
        arecv=pltpu.VMEM((NZ, BLOCKS, DOWN, RANKS), BF16),
        c0=pltpu.VMEM((NX, NY, 2, ROWS, HALF), BF16),
        c1=pltpu.VMEM((NX, NY, 2, ROWS, HALF), BF16),
        pa=pltpu.VMEM((NX, NY, ROWS, HALF), BF16),
        pb=pltpu.VMEM((NY, NX, ROWS, HALF), BF16),
        ra1=pltpu.VMEM((3, NY, ROWS, HALF), BF16),
        rb1=pltpu.VMEM((3, NX, ROWS, HALF), BF16),
        qa=pltpu.VMEM((NY, ROWS, HALF), BF16),
        qb=pltpu.VMEM((NX, ROWS, HALF), BF16),
        ra2=pltpu.VMEM((3, ROWS, HALF), BF16),
        rb2=pltpu.VMEM((3, ROWS, HALF), BF16),
        lg=pltpu.VMEM((NX, NY, 2, ROWS, RANKS), BF16),
        lp=pltpu.VMEM((NX, NY, 2, ROWS, RANKS), BF16),
        lr=pltpu.VMEM((7, NY, ROWS, RANKS), BF16),
        lq=pltpu.VMEM((NY, ROWS, RANKS), BF16),
        ls=pltpu.VMEM((3, ROWS, RANKS), BF16),
        la=pltpu.VMEM((NX, NY, 2, ROWS, RANKS), BF16),
        gasend=pltpu.VMEM((NZ, BLOCKS, DOWN, RANKS), BF16),
        garecv=pltpu.VMEM((NZ, BLOCKS, DOWN, RANKS), BF16),
        gbf=pltpu.VMEM((NZ, DOWN, RANKS), F32),
        gbsend=pltpu.VMEM((NZ, DOWN, RANKS), BF16),
        gbrecv=pltpu.VMEM((NZ, DOWN, RANKS), BF16),
        tga=pltpu.VMEM((NZ, 1, RANKS), I32),
        tgb=pltpu.VMEM((2, 1, NZ * DOWN), I32),
        gaacc=pltpu.VMEM((SLOTS * DOWN, RANKS), F32),
        gbt=pltpu.VMEM((UP, COLS, SLOTS), F32),
        igv=pltpu.VMEM((NX, NY * 2 * ROWS, FEATS), BF16),
        kvv=pltpu.VMEM((ROWS, WIDTH), BF16),
        loc=pltpu.SemaphoreType.DMA((12,)),
        zs=pltpu.SemaphoreType.DMA((4, NZ)),
        zr=pltpu.SemaphoreType.DMA((4, NZ)),
        ps=pltpu.SemaphoreType.DMA((80,)),
        pr=pltpu.SemaphoreType.DMA((80,)),
    )


def kern(names, ten, slot, x_h, w_h, ad_h, au_h, cot_h, kv_o, ig_o, ga_o, gb_o, *refs):
    s = dict(zip(names, refs, strict=True))
    z, x, t = lax.axis_index("dp"), lax.axis_index("pipe"), lax.axis_index("tensor")
    y, c = lax.div(t, 2), lax.rem(t, 2)
    own_block = x * 2 + lax.div(y, 2)
    quarter = lax.rem(t, 4)

    locals_ = {}

    def local(name, src, dst, i):
        cp = pltpu.make_async_copy(src, dst, s["loc"].at[i])
        cp.start()
        locals_[name] = cp

    local("au", au_h, s["au"], 0)
    local("ad", ad_h, s["ad"], 1)
    local("c0", cot_h.at[:, pl.ds(0, HALF)], s["c0"].at[x, y, c], 2)
    local("c1", cot_h.at[:, pl.ds(HALF, HALF)], s["c1"].at[x, y, c], 3)
    local("x", x_h, s["xv"], 4)
    local("w", w_h, s["wv"], 5)

    def at_z(d):
        return (lax.rem(z + d, NZ), x, t)

    def at_xc(dx, dc):
        xd = lax.rem(x + dx, NX)
        cd = c if dc == 0 else 1 - c
        return xd, cd, (z, xd, 2 * y + cd)

    def at_y(dy):
        yd = lax.rem(y + dy, NY)
        return yd, (z, x, 2 * yd + c)

    def dist(k):
        half = lax.div(k + 1, 2)
        return 8 + half * (1 - 2 * lax.rem(k, 2))

    partner = (z, x, 2 * y + 1 - c)
    y1 = y + 1 - 2 * lax.rem(y, 2)
    quads = [partner, (z, x, 2 * y1 + c), (z, x, 2 * y1 + 1 - c)]
    quad_sem = [1, 2, 3]
    rows7 = [(dx, dc) for dx in range(NX) for dc in range(2) if (dx, dc) != (0, 0)]

    barrier = pltpu.get_barrier_semaphore()

    def hello(dev):
        pl.semaphore_signal(barrier, inc=1, device_id=dev, device_id_type=MESH)

    @pl.loop(0, NZ - 1)
    def _(k):
        hello(at_z(dist(k)))

    for dx, dc in rows7:
        hello(at_xc(dx, dc)[2])
    for dy in range(1, NY):
        hello(at_y(dy)[1])
    hello(quads[2])

    counter = [0]
    sent = []

    def take(n):
        first = counter[0]
        counter[0] += n
        return first

    def copy(src, dst, dev, i):
        return pltpu.make_async_remote_copy(
            src_ref=src,
            dst_ref=dst,
            send_sem=s["ps"].at[i],
            recv_sem=s["pr"].at[i],
            device_id=dev,
            device_id_type=MESH,
        )

    def push(cps):
        for cp in cps:
            cp.start()
            sent.append(cp)
        return cps

    def arrived(cps):
        for cp in cps:
            cp.wait_recv()

    def z_copy(kind, src, dst, d):
        return pltpu.make_async_remote_copy(
            src_ref=src,
            dst_ref=dst.at[z],
            send_sem=s["zs"].at[kind, d],
            recv_sem=s["zr"].at[kind, d],
            device_id=at_z(d),
            device_id_type=MESH,
        )

    def z_send(kind, src, dst):
        @pl.loop(0, NZ - 1)
        def _(k):
            d = dist(k)
            z_copy(kind, src.at[lax.rem(z + d, NZ)], dst, d).start()

    def z_wait(kind, src, dst):
        @pl.loop(0, NZ - 1)
        def _(k):
            z_copy(kind, src.at[0], dst, dist(k)).wait_recv()

    def slot_of(b):
        return slot[ten[b]]

    locals_["au"].wait()

    @pl.loop(0, NZ)
    def _(zd):
        row = slot_of(zd * BLOCKS + own_block)
        lanes = pl.ds(pl.multiple_of(quarter * QUARTER, QUARTER), QUARTER)
        s["bsend"][zd] = s["au"][row, :, lanes]

    locals_["ad"].wait()
    lane = lax.broadcasted_iota(I32, (1, RANKS), 1)
    lane2 = lax.broadcasted_iota(I32, (1, NZ * DOWN), 1)

    def gather(zd, carry):
        b_lo, b_hi = carry
        tg = jnp.zeros((1, RANKS), I32)
        for b in range(BLOCKS):
            row = slot_of(zd * BLOCKS + b)
            s["asend"][zd, b] = s["ad"][row]
            tg = jnp.where(lax.div(lane, DOWN) == b, row * DOWN + lax.rem(lane, DOWN), tg)
            here = lax.div(lane2, UP) == zd * UP + b % 4
            mine = lax.rem(lane2, UP) * SLOTS + row
            if b < 4:
                b_lo = jnp.where(here, mine, b_lo)
            else:
                b_hi = jnp.where(here, mine, b_hi)
        s["tga"][zd] = tg
        return b_lo, b_hi

    zero2 = jnp.zeros((1, NZ * DOWN), I32)
    tgb_lo, tgb_hi = lax.fori_loop(0, NZ, gather, (zero2, zero2))
    s["tgb"][0] = tgb_lo
    s["tgb"][1] = tgb_hi
    locals_["c0"].wait()
    locals_["c1"].wait()
    locals_["x"].wait()
    locals_["w"].wait()
    pl.semaphore_wait(barrier, NZ - 1 + 7 + 3 + 1)

    z_send(0, s["bsend"], s["brecv"])
    z_send(1, s["asend"], s["arecv"])
    i0 = take(2)
    pair = push(
        [
            copy(s["xv"].at[:, :, 1 - c], s["xp"], partner, i0),
            copy(s["wv"], s["wp"], partner, i0 + 1),
        ]
    )
    c0, c1 = s["c0"], s["c1"]
    i0 = take(6)
    cot1a = push(
        [
            copy(c0.at[x, y, c], c0.at[x, y, c], at_xc(d, 0)[2], i0 + d - 1)
            for d in range(1, NX)
        ]
    )
    cot1b = push(
        [
            copy(c1.at[x, y, c], c1.at[x, y, c], at_y(d)[1], i0 + 2 + d)
            for d in range(1, NY)
        ]
    )
    s["brecv"][z] = s["bsend"][z]
    s["arecv"][z] = s["asend"][z]

    arrived(pair)
    x_own = s["xv"].at[:, :, c][...].reshape(NX * NY * ROWS, FEATS)
    x_other = s["xp"][...].reshape(NX * NY * ROWS, FEATS)

    def project(j):
        cols = slice(j * QUARTER, (j + 1) * QUARTER)
        v = jnp.dot(x_own, s["wv"][:, cols], preferred_element_type=F32)
        v = v + jnp.dot(x_other, s["wp"][:, cols], preferred_element_type=F32)
        v = v.astype(BF16).reshape(NX, NY, ROWS, QUARTER)
        if j < 2:
            s["pa"][:, :, :, cols] = v
        else:
            cols = slice((j - 2) * QUARTER, (j - 1) * QUARTER)
            for xx in range(NX):
                s["pb"][:, xx, :, cols] = v[xx]

    project(0)
    project(1)
    i0 = take(3)
    rs1a = push(
        [
            copy(s["pa"].at[at_xc(d, 0)[0]], s["ra1"].at[d - 1], at_xc(d, 0)[2], i0 + d - 1)
            for d in range(1, NX)
        ]
    )
    project(2)
    project(3)

    z_wait(0, s["bsend"], s["brecv"])
    for k in range(NZ):
        s["bqf"][k * UP : (k + 1) * UP, :] = s["brecv"][k].astype(F32)
    s["bown"][quarter] = s["bqf"][...].astype(BF16)
    i0 = take(3)
    quad = push(
        [
            copy(s["bown"].at[quarter], s["bown"].at[quarter], dev, i0 + n - 1)
            for n, dev in zip(quad_sem, quads, strict=True)
        ]
    )
    arrived(quad)
    last = (((1,), (1,)), ((), ()))

    def back(ref, first):
        v = ref[x, y, c]
        a = lax.dot_general(v[:, :QUARTER], s["bown"][first], last, preferred_element_type=F32)
        b = lax.dot_general(v[:, QUARTER:], s["bown"][first + 1], last, preferred_element_type=F32)
        return a + b

    lg, la = s["lg"], s["la"]
    lg[x, y, c] = jnp.concatenate([back(c0, 0), back(c1, 2)], axis=1).astype(BF16)

    def gather_y(ref):
        i0 = take(3)
        return push(
            [
                copy(ref.at[x, y, c], ref.at[x, y, c], at_y(d)[1], i0 + d - 1)
                for d in range(1, NY)
            ]
        )

    def gather_x(ref):
        i0 = take(7)
        return push(
            [
                copy(ref.at[x, :, c], ref.at[x, :, c], at_xc(dx, dc)[2], i0 + n)
                for n, (dx, dc) in enumerate(rows7)
            ]
        )

    lgy = gather_y(lg)
    arrived(cot1a)
    i0 = take(3)
    cot2a = push(
        [
            copy(c0.at[:, y, c], c0.at[:, y, c], at_y(d)[1], i0 + d - 1)
            for d in range(1, NY)
        ]
    )
    i0 = take(3)
    rs1b = push(
        [
            copy(s["pb"].at[at_y(d)[0]], s["rb1"].at[d - 1], at_y(d)[1], i0 + d - 1)
            for d in range(1, NY)
        ]
    )
    arrived(lgy)
    lgx = gather_x(lg)
    arrived(cot1b)
    i0 = take(3)
    cot2b = push(
        [
            copy(c1.at[x, :, c], c1.at[x, :, c], at_xc(d, 0)[2], i0 + d - 1)
            for d in range(1, NX)
        ]
    )
    i3 = take(8)
    cot3 = push(
        [
            copy(c0.at[:, y, c], c0.at[:, y, c], partner, i3),
            copy(c1.at[x, :, c], c1.at[x, :, c], partner, i3 + 4),
        ]
    )

    def tok(b):
        return s["xv"][lax.div(b, 2), pl.ds(2 * lax.rem(b, 2), 2)].reshape(4 * ROWS, FEATS)

    def low_of(ref, b):
        return ref[lax.div(b, 2), pl.ds(2 * lax.rem(b, 2), 2)].reshape(4 * ROWS, RANKS)

    def down_of(b):
        return s["arecv"][:, b].reshape(FEATS, RANKS)

    first = (((0,), (0,)), ((), ()))
    arrived(lgx)

    @pl.loop(0, BLOCKS)
    def _(b):
        v = lax.dot_general(tok(b), low_of(lg, b), first, preferred_element_type=F32)
        s["gasend"][:, b] = v.astype(BF16).reshape(NZ, DOWN, RANKS)

    z_send(2, s["gasend"], s["garecv"])
    s["garecv"][z] = s["gasend"][z]

    z_wait(1, s["asend"], s["arecv"])
    lp = s["lp"]

    @pl.loop(0, BLOCKS)
    def _(b):
        v = jnp.dot(tok(b), down_of(b), preferred_element_type=F32)
        lp[lax.div(b, 2), pl.ds(2 * lax.rem(b, 2), 2)] = v.astype(BF16).reshape(2, 2, ROWS, RANKS)

    i0 = take(7)
    lowx = push(
        [
            copy(
                lp.at[at_xc(dx, dc)[0], :, at_xc(dx, dc)[1]],
                s["lr"].at[n],
                at_xc(dx, dc)[2],
                i0 + n,
            )
            for n, (dx, dc) in enumerate(rows7)
        ]
    )

    def total(own, ref, n):
        v = own.astype(F32)
        for k in range(n):
            v = v + ref[k].astype(F32)
        return v

    arrived(rs1a)
    for yy in range(NY):
        v = total(s["pa"][x, yy], s["ra1"].at[:, yy], 3)
        s["qa"][yy] = v.astype(BF16)
    arrived(lowx)
    s["lq"][...] = total(lp.at[x, :, c][...], s["lr"], 7).astype(BF16)
    i0 = take(3)
    lowy = push(
        [
            copy(s["lq"].at[at_y(d)[0]], s["ls"].at[d - 1], at_y(d)[1], i0 + d - 1)
            for d in range(1, NY)
        ]
    )
    i0 = take(3)
    rs2a = push(
        [
            copy(s["qa"].at[at_y(d)[0]], s["ra2"].at[d - 1], at_y(d)[1], i0 + d - 1)
            for d in range(1, NY)
        ]
    )
    arrived(lowy)
    low_rows = total(s["lq"][y], s["ls"], 3).astype(BF16)
    la[x, y, c] = low_rows
    lay = gather_y(la)
    for d in range(1, NY):
        cot2a[d - 1].wait_recv()
        src = lax.rem(y - d + NY, NY)
        cot3 += push([copy(c0.at[:, src, c], c0.at[:, src, c], partner, i3 + d)])
    arrived(lay)
    lax_ = gather_x(la)
    for d in range(1, NX):
        cot2b[d - 1].wait_recv()
        src = lax.rem(x - d + NX, NX)
        cot3 += push([copy(c1.at[src, :, c], c1.at[src, :, c], partner, i3 + 4 + d)])
    arrived(rs1b)
    for xx in range(NX):
        v = total(s["pb"][y, xx], s["rb1"].at[:, xx], 3)
        s["qb"][xx] = v.astype(BF16)
    i0 = take(3)
    rs2b = push(
        [
            copy(s["qb"].at[at_xc(d, 0)[0]], s["rb2"].at[d - 1], at_xc(d, 0)[2], i0 + d - 1)
            for d in range(1, NX)
        ]
    )
    arrived(lax_)
    arrived(cot3)

    group = x * 8 + t
    chunk = pl.ds(pl.multiple_of(lax.rem(lax.div(group, 2), 8) * 128, 128), 128)
    values = lax.div(group, 16)

    def cot_cols(b):
        at = (lax.div(b, 2), pl.ds(2 * lax.rem(b, 2), 2), slice(None), slice(None), chunk)
        v = jnp.where(values == 0, c0[at].astype(F32), c1[at].astype(F32))
        return v.astype(BF16).reshape(4 * ROWS, 128)

    wide = lax.broadcasted_iota(I32, (COLS, 128), 1)

    def up_part(b):
        v = lax.dot_general(low_of(la, b), cot_cols(b), first, preferred_element_type=F32)
        v = jnp.where(values == 0, v[:COLS], v[COLS:])
        return v, pltpu.roll(v, COLS, 1)

    for b4 in range(4):
        lo, lo_r = up_part(b4)
        hi, hi_r = up_part(b4 + 4)
        left = jnp.where(c == 0, lo, lo_r)
        right = jnp.where(c == 0, hi_r, hi)
        v = jnp.where(wide < COLS, left, right)
        for k in range(NZ):
            s["gbf"][k, b4 * UP : (b4 + 1) * UP, :] = v[k * UP : (k + 1) * UP]
    s["gbsend"][...] = s["gbf"][...].astype(BF16)
    z_send(3, s["gbsend"], s["gbrecv"])
    s["gbrecv"][z] = s["gbsend"][z]

    @pl.loop(0, NX)
    def _(xx):
        rows = NY * 2 * ROWS
        v = lax.dot_general(
            c0[xx].reshape(rows, HALF), s["wv"][:, :HALF], last, preferred_element_type=F32
        )
        v = v + lax.dot_general(
            c1[xx].reshape(rows, HALF), s["wv"][:, HALF:], last, preferred_element_type=F32
        )
        low = [
            lax.dot_general(low_of(lg, 2 * xx + k), down_of(2 * xx + k), last, preferred_element_type=F32)
            for k in range(2)
        ]
        s["igv"][xx] = (v + jnp.concatenate(low, axis=0)).astype(BF16)

    local("ig", s["igv"], ig_o, 6)

    arrived(rs2a)
    arrived(rs2b)
    low_rows = la[x, y, c]
    for j in range(4):
        cols = slice((j % 2) * QUARTER, (j % 2 + 1) * QUARTER)
        if j < 2:
            own, r1, r2 = s["pa"][x, y, :, cols], s["ra1"].at[:, y, :, cols], s["ra2"].at[:, :, cols]
        else:
            own, r1, r2 = s["pb"][y, x, :, cols], s["rb1"].at[:, x, :, cols], s["rb2"].at[:, :, cols]
        side = low_rows[:, :COLS] if j < 2 else low_rows[:, COLS:]
        v = total(total(own, r1, 3), r2, 3)
        v = v + jnp.dot(side, s["bown"][j], preferred_element_type=F32)
        s["kvv"][:, j * QUARTER : (j + 1) * QUARTER] = v.astype(BF16)
    local("kv", s["kvv"], kv_o, 7)

    def pick(ref, kind, dst, ks):
        for k in ks:
            z_copy(kind, ref.at[0], dst, k).wait_recv()

    order = [0] + [8 + ((k + 1) // 2) * (1 - 2 * (k % 2)) for k in range(NZ - 1)]
    high = 128
    for part in range(4):
        ds = order[4 * part : 4 * part + 4]
        pick(s["gasend"], 2, s["garecv"], [d for d in ds if d])
        srcs = [lax.rem(z - d + NZ, NZ) for d in ds]
        tg = jnp.concatenate([s["tga"][k] for k in srcs], axis=1)
        data = jnp.concatenate([s["garecv"][k].reshape(BLOCKS * DOWN, RANKS) for k in srcs], axis=0)

        @pl.loop(0, SLOTS * DOWN // high)
        def _(r, part=part, tg=tg, data=data):
            at = pl.ds(pl.multiple_of(r * high, high), high)
            ids = lax.broadcasted_iota(I32, (high, 4 * RANKS), 0) + r * high
            sel = jnp.where(ids == tg, 1.0, 0.0).astype(BF16)
            v = jnp.dot(sel, data, preferred_element_type=F32)
            if part:
                v = v + s["gaacc"][at, :]
            s["gaacc"][at, :] = v

    local("ga", s["gaacc"], ga_o, 8)
    z_wait(3, s["gbsend"], s["gbrecv"])
    data = s["gbrecv"][...].reshape(NZ * DOWN, RANKS)
    ids = lax.broadcasted_iota(I32, (UP * SLOTS, NZ * DOWN), 0)
    sums = []
    for h in range(2):
        sel = jnp.where(ids == s["tgb"][h], 1.0, 0.0).astype(BF16)
        sums.append(jnp.dot(sel, data, preferred_element_type=F32))
    for i in range(UP):
        at = slice(i * SLOTS, (i + 1) * SLOTS)
        lo, hi = sums[0][at].T, sums[1][at].T
        s["gbt"][i] = lo[:COLS] + hi[COLS:]
    local("gb", s["gbt"], gb_o, 9)

    for cp in sent:
        cp.wait_send()

    @pl.loop(1, NZ)
    def _(d):
        z_copy(0, s["bsend"].at[0], s["brecv"], d).wait_send()
        z_copy(1, s["asend"].at[0], s["arecv"], d).wait_send()
        z_copy(2, s["gasend"].at[0], s["garecv"], d).wait_send()
        z_copy(3, s["gbsend"].at[0], s["gbrecv"], d).wait_send()

    for name in ("ig", "kv", "ga", "gb"):
        locals_[name].wait()


def body(tokens, weight, down, up, tenant_of_block, slot_of_tenant, cotangent):
    sc = scratches()
    anywhere = pl.BlockSpec(memory_space=pl.ANY)
    scalars = pl.BlockSpec(memory_space=pltpu.SMEM)
    kv, ig, ga, gb = pl.pallas_call(
        functools.partial(kern, tuple(sc)),
        out_shape=(
            jax.ShapeDtypeStruct((ROWS, WIDTH), BF16),
            jax.ShapeDtypeStruct((NX, NY * 2 * ROWS, FEATS), BF16),
            jax.ShapeDtypeStruct((SLOTS * DOWN, RANKS), F32),
            jax.ShapeDtypeStruct((UP, COLS, SLOTS), F32),
        ),
        in_specs=[scalars] * 2 + [anywhere] * 5,
        out_specs=(anywhere,) * 4,
        scratch_shapes=list(sc.values()),
        compiler_params=pltpu.CompilerParams(
            collective_id=0, has_side_effects=True, vmem_limit_bytes=60 * 1024 * 1024
        ),
    )(
        tenant_of_block,
        slot_of_tenant,
        tokens.reshape(NX, NY, 2, ROWS, FEATS),
        weight,
        down,
        up,
        cotangent,
    )
    return (
        kv,
        ig.reshape(NX * NY * 2 * ROWS, FEATS),
        ga.reshape(SLOTS, DOWN, RANKS),
        gb.transpose(2, 0, 1),
    )


def solution(mesh):
    placed = (
        P("dp", ("pipe", "tensor")),
        P(("pipe", "tensor"), None),
        P(None, ("pipe", "tensor", "dp"), None),
        P(None, "dp", None),
        P(),
        P(),
        P(("dp", "pipe", "tensor"), None),
    )
    return jax.shard_map(
        body,
        mesh=mesh,
        in_specs=placed,
        out_specs=(
            P(("dp", "pipe", "tensor"), None),
            P("dp", ("pipe", "tensor")),
            P(None, ("pipe", "tensor", "dp"), None),
            P(None, "dp", ("pipe", "tensor")),
        ),
        check_vma=False,
    )
```

time: 396 us -> 92.8 us (0.23)
  waiting for transfers between devices: 240 us -> 0 us
  blocking collectives: 95 us -> 0 us
  Pallas kernels: 0 us -> 86.9 us
  starting transfers between devices: 17.7 us -> 0 us
  matrix products: 15.1 us -> 0 us
  between operations: 14 us -> 0.66 us
  local copies, waits for them, and re-layouts: 10.2 us -> 5.06 us
    reduce_scatter x1 -> x0, waiting for transfers between devices: 104 us -> none  [body(): lax.psum_scatter(jnp.dot(tokens, key_value_weight, preferred_element_type...]
    pallas_call x0 -> x1, Pallas kernels: none -> 86.9 us  [body(): pl.pallas_call(functools.partial(kern, tuple(sc)), out_shape=(jax.ShapeDt...]
    all_gather x1 -> x0, waiting for transfers between devices: 64.5 us -> none  [body(): lax.all_gather(cotangent, ('pipe', 'tensor'), axis=0, tiled=True)]
    all_to_all x2 -> x0, blocking collectives: 64.5 us -> none  [the longest x1 38.5 us: body(): lax.all_to_all(a_send, 'dp', split_axis=0, concat_axis=1, tiled=True)]
    psum x1 -> x0, waiting for transfers between devices: 63.9 us -> none  [body(): low_all = lax.psum(low_part.astype(jnp.bfloat16), ('pipe', 'tensor'))]
    all_gather x1 -> x0, blocking collectives: 30.5 us -> none  [body(): lax.all_gather(grad_rows, ('pipe', 'tensor'), axis=0, tiled=True)]
    all_to_all x2 -> x0, starting transfers between devices: 17.5 us -> none  [the longest x1 12 us: body(): lax.all_to_all(grad_b_part.astype(jnp.bfloat16), 'dp', split_axis=1, conc...]
    dot_general x14 -> x0, matrix products: 15.1 us -> none  [the longest x1 4.27 us: body(): lax.dot_general(cot_all, key_value_weight, contract_last, preferred_eleme...]
  transfers between devices with their start and end apart: 5 -> 0, of which waited for: 4 -> 0; matrix products, arithmetic and copies ran while one was open for 5% -> 0% of each run, Pallas kernels for 0% -> 0%
where the time goes in v1:
time: 92.8 us; the launch traced here: 92.6 us
  Pallas kernels  86.9 us (94%)
  local copies, waits for them, and re-layouts  5.06 us (5%)
    pallas_call x1, Pallas kernels, body(): pl.pallas_call(functools.partial(kern, tuple(sc)), out_shape=(jax.ShapeDt...  86.9 us
    unnamed x8, local copies, waits for them, and re-layouts  5.06 us

profile of v1, /device:TPU:1, one launch (start us, length us, event | category | flops | bytes accessed | tf_op | source)
XLA Modules:
  0.0 92.6 jit_solution(7180048054958756345)
XLA Ops:
  0.6 86.9 %shard_map.102 = (bf16[32,2048]{1,0:T(8,128)(2,1)}, bf16[4,256,256]{2,1,0:T(8,128)(2,1)}, f32[1536,128]{1,0:T(8,128)}, f32[4,64,96]{2,1,0:T(8,128)}) custom-call(s32[128]{0:T(128)} %ten.1, s32[96]{0:T(128)} %slot.1, bf16[4,4,2,32,256]{4,3,2,1,0:T(8,128)(2,1)} %bitcast.6, bf16[256,2048]{1,0:T(8,128)(2,1)} %w_h.1, bf16[96,16,128]{2,1,0:T(8,128)(2,1)} %ad_h.1, ...), custom_call_target="tpu_custom_call" | custom-call | tf_op jit(solution)/shard_map/pallas_call | solution.py:555
  87.5 0.0 copy-start
  87.5 0.0 copy-start.1
  87.6 1.6 %copy.15 = bf16[32,2048]{1,0:T(8,128)(2,1)} copy(bf16[32,2048]{1,0:T(8,128)(2,1)} %get-tuple-element.16) | data formatting | bytes 262144
  89.2 1.9 %copy.16 = bf16[1024,256]{1,0:T(8,128)(2,1)} copy(bf16[1024,256]{1,0:T(8,128)(2,1)} %bitcast.5) | data formatting | bytes 1048576
  91.1 0.0 copy-done
  91.1 0.9 copy.17
  92.0 0.0 copy-done.1
  92.0 0.7 copy.18
Async XLA Ops:
  87.5 3.5 %copy-start = (f32[1536,128]{1,0:T(8,128)S(1)}, f32[1536,128]{1,0:T(8,128)}, u32[]{:S(2)}) copy-start(f32[1536,128]{1,0:T(8,128)} %get-tuple-element.10) | copy-start | bytes 2359300
  87.5 4.4 %copy-start.1 = (f32[4,64,96]{2,1,0:T(8,128)S(1)}, f32[4,64,96]{2,1,0:T(8,128)}, u32[]{:S(2)}) copy-start(f32[4,64,96]{2,1,0:T(8,128)} %get-tuple-element.11) | copy-start | bytes 294916

commit v2 on v1

v2 whole, which is shorter than its diff:
```python
import functools

import jax
import jax.numpy as jnp
from jax import lax
from jax.experimental import pallas as pl
from jax.experimental.pallas import tpu as pltpu
from jax.sharding import PartitionSpec as P

MESH = pl.DeviceIdType.MESH
F32, BF16, I32 = jnp.float32, jnp.bfloat16, jnp.int32
NZ, NX, NY = 16, 4, 4
SLOTS, UP, DOWN, RANKS = 96, 4, 16, 128
BLOCKS = 8
ROWS, FEATS, WIDTH, HALF, QUARTER = 32, 256, 2048, 1024, 512
COLS = 64
GROUPS = 29


def scratches():
    return dict(
        au=pltpu.VMEM((SLOTS, UP, WIDTH), BF16),
        ad=pltpu.VMEM((SLOTS, DOWN, RANKS), BF16),
        xv=pltpu.VMEM((NX, NY, 2, ROWS, FEATS), BF16),
        wv=pltpu.VMEM((FEATS, WIDTH), BF16),
        xp=pltpu.VMEM((NX, NY, ROWS, FEATS), BF16),
        wp=pltpu.VMEM((FEATS, WIDTH), BF16),
        bsend=pltpu.VMEM((NZ, UP, QUARTER), BF16),
        brecv=pltpu.VMEM((NZ, UP, QUARTER), BF16),
        bqf=pltpu.VMEM((NZ * UP, QUARTER), F32),
        bown=pltpu.VMEM((4, NZ * UP, QUARTER), BF16),
        asend=pltpu.VMEM((NZ, BLOCKS, DOWN, RANKS), BF16),
        arecv=pltpu.VMEM((NZ, BLOCKS, DOWN, RANKS), BF16),
        c0=pltpu.VMEM((NX, NY, 2, ROWS, HALF), BF16),
        c1=pltpu.VMEM((NX, NY, 2, ROWS, HALF), BF16),
        pa=pltpu.VMEM((NX, NY, ROWS, HALF), BF16),
        pb=pltpu.VMEM((NY, NX, ROWS, HALF), BF16),
        ra1=pltpu.VMEM((3, NY, ROWS, HALF), BF16),
        rb1=pltpu.VMEM((3, NX, ROWS, HALF), BF16),
        qa=pltpu.VMEM((NY, ROWS, HALF), BF16),
        qb=pltpu.VMEM((NX, ROWS, HALF), BF16),
        ra2=pltpu.VMEM((3, ROWS, HALF), BF16),
        rb2=pltpu.VMEM((3, ROWS, HALF), BF16),
        cq=pltpu.VMEM((4, ROWS, QUARTER), BF16),
        phs=pltpu.VMEM((COLS, RANKS), F32),
        phr=pltpu.VMEM((COLS, RANKS), F32),
        lgp=pltpu.VMEM((NX, NY, COLS, RANKS), BF16),
        lgm=pltpu.VMEM((BLOCKS, 4 * ROWS, RANKS), BF16),
        lp=pltpu.VMEM((NX, NY, 2, ROWS, RANKS), BF16),
        lr=pltpu.VMEM((7, NY, ROWS, RANKS), BF16),
        lq=pltpu.VMEM((NY, ROWS, RANKS), BF16),
        ls=pltpu.VMEM((3, ROWS, RANKS), BF16),
        la=pltpu.VMEM((NX, NY, 2, ROWS, RANKS), BF16),
        gaf=pltpu.VMEM((FEATS * BLOCKS, RANKS), F32),
        gasend=pltpu.VMEM((NZ, BLOCKS, DOWN * RANKS), BF16),
        garecv=pltpu.VMEM((NZ, BLOCKS, DOWN * RANKS), BF16),
        gbf=pltpu.VMEM((NZ, DOWN, RANKS), F32),
        gbsend=pltpu.VMEM((NZ, DOWN, RANKS), BF16),
        gbrecv=pltpu.VMEM((NZ, DOWN, RANKS), BF16),
        tga=pltpu.VMEM((1, NZ * BLOCKS), I32),
        tgb=pltpu.VMEM((2, 1, NZ * DOWN), I32),
        ten=pltpu.SMEM((NZ * BLOCKS,), I32),
        slot=pltpu.SMEM((SLOTS,), I32),
        loc=pltpu.SemaphoreType.DMA((13,)),
        zs=pltpu.SemaphoreType.DMA((4,)),
        zr=pltpu.SemaphoreType.DMA((4,)),
        ps=pltpu.SemaphoreType.DMA((GROUPS,)),
        pr=pltpu.SemaphoreType.DMA((GROUPS,)),
    )


def kern(names, ten_h, slot_h, x_h, w_h, ad_h, au_h, cot_h, kv_o, ig_o, ga_o, gb_o, *refs):
    s = dict(zip(names, refs, strict=True))
    z, x, t = lax.axis_index("dp"), lax.axis_index("pipe"), lax.axis_index("tensor")
    y, c = lax.div(t, 2), lax.rem(t, 2)
    own_block = x * 2 + lax.div(y, 2)
    quarter = lax.rem(t, 4)

    locals_ = {}

    def quarter_lanes(q):
        return pl.ds(pl.multiple_of(q * QUARTER, QUARTER), QUARTER)

    def local(name, src, dst, i):
        cp = pltpu.make_async_copy(src, dst, s["loc"].at[i])
        cp.start()
        locals_[name] = cp

    def at_z(d):
        return (lax.rem(z + d, NZ), x, t)

    def at_xc(dx, dc):
        xd = lax.rem(x + dx, NX)
        cd = c if dc == 0 else 1 - c
        return xd, cd, (z, xd, 2 * y + cd)

    def at_y(dy):
        yd = lax.rem(y + dy, NY)
        return yd, (z, x, 2 * yd + c)

    def dist(k):
        half = lax.div(k + 1, 2)
        return 8 + half * (1 - 2 * lax.rem(k, 2))

    partner = (z, x, 2 * y + 1 - c)
    y1 = y + 1 - 2 * lax.rem(y, 2)
    quad_of = [quarter + 1 - 2 * c, lax.rem(quarter + 2, 4), lax.rem(quarter + 3 - 2 * c, 4)]
    quads = [partner, (z, x, 2 * y1 + c), (z, x, 2 * y1 + 1 - c)]
    rows7 = [(dx, dc) for dx in range(NX) for dc in range(2) if (dx, dc) != (0, 0)]

    barrier = pltpu.get_barrier_semaphore()

    def hello(dev):
        pl.semaphore_signal(barrier, inc=1, device_id=dev, device_id_type=MESH)

    @pl.loop(0, NZ - 1)
    def _(k):
        hello(at_z(dist(k)))

    for dx, dc in rows7:
        hello(at_xc(dx, dc)[2])
    for dy in range(1, NY):
        hello(at_y(dy)[1])
    hello(quads[2])
    local("ten", ten_h, s["ten"], 10)
    local("slot", slot_h, s["slot"], 11)
    local("au", au_h, s["au"], 0)
    local("ad", ad_h, s["ad"], 1)
    local("c0", cot_h.at[:, pl.ds(0, HALF)], s["c0"].at[x, y, c], 2)
    local("c1", cot_h.at[:, pl.ds(HALF, HALF)], s["c1"].at[x, y, c], 3)
    local("cq", cot_h.at[:, quarter_lanes(quarter)], s["cq"].at[quarter], 9)
    local("x", x_h, s["xv"], 4)
    local("w", w_h, s["wv"], 5)

    groups = []

    def until(ref, sem):
        pltpu.make_async_copy(ref, ref, sem).wait()

    def push(like, *copies):
        i = len(groups)
        groups.append(like)
        for src, dst, dev in copies:
            pltpu.make_async_remote_copy(
                src_ref=src,
                dst_ref=dst,
                send_sem=s["ps"].at[i],
                recv_sem=s["pr"].at[i],
                device_id=dev,
                device_id_type=MESH,
            ).start()
        return i

    def arrived(*ids):
        for i in ids:
            until(groups[i], s["pr"].at[i])

    def z_send(kind, src, dst, lo=0, hi=NZ - 1):
        @pl.loop(lo, hi)
        def _(k):
            d = dist(k)
            pltpu.make_async_remote_copy(
                src_ref=src.at[lax.rem(z + d, NZ)],
                dst_ref=dst.at[z],
                send_sem=s["zs"].at[kind],
                recv_sem=s["zr"].at[kind],
                device_id=at_z(d),
                device_id_type=MESH,
            ).start()

    def z_wait(kind, ref):
        until(ref.at[pl.ds(0, NZ - 1)], s["zr"].at[kind])

    def slot_of(b):
        return s["slot"][s["ten"][b]]

    locals_["ten"].wait()
    locals_["slot"].wait()
    locals_["au"].wait()

    @pl.loop(0, NZ)
    def _(zd):
        row = slot_of(zd * BLOCKS + own_block)
        s["bsend"][zd] = s["au"][row, :, quarter_lanes(quarter)]

    locals_["ad"].wait()
    lane = lax.broadcasted_iota(I32, (1, RANKS), 1)
    lane2 = lax.broadcasted_iota(I32, (1, NZ * DOWN), 1)

    def gather(zd, carry):
        slots, b_lo, b_hi = carry
        for b in range(BLOCKS):
            row = slot_of(zd * BLOCKS + b)
            s["asend"][zd, b] = s["ad"][row]
            slots = jnp.where(lane == zd * BLOCKS + b, row, slots)
            here = lax.div(lane2, UP) == zd * UP + b % 4
            mine = lax.rem(lane2, UP) * SLOTS + row
            if b < 4:
                b_lo = jnp.where(here, mine, b_lo)
            else:
                b_hi = jnp.where(here, mine, b_hi)
        return slots, b_lo, b_hi

    zero2 = jnp.zeros((1, NZ * DOWN), I32)
    zero1 = jnp.zeros((1, NZ * BLOCKS), I32)
    s["tga"][...], s["tgb"][0], s["tgb"][1] = lax.fori_loop(0, NZ, gather, (zero1, zero2, zero2))
    locals_["c0"].wait()
    locals_["c1"].wait()
    locals_["x"].wait()
    locals_["w"].wait()
    pl.semaphore_wait(barrier, NZ - 1 + 7 + 3 + 1)

    c0, c1, lgp, la, lp = s["c0"], s["c1"], s["lgp"], s["la"], s["lp"]
    piece = s["ra1"]
    z_send(0, s["bsend"], s["brecv"])
    z_send(1, s["asend"], s["arecv"])
    pair = [
        push(s["xp"], (s["xv"].at[:, :, 1 - c], s["xp"], partner)),
        push(s["wp"], (s["wv"], s["wp"], partner)),
    ]
    own0, own1 = c0.at[x, y, c], c1.at[x, y, c]
    cot1 = [
        push(s["ra2"], *[(own0, own0, at_xc(d, 0)[2]) for d in (1, 3, 2)]),
        push(s["rb2"], *[(own1, own1, at_y(d)[1]) for d in (1, 3, 2)]),
    ]
    quad_rows = push(
        s["cq"].at[pl.ds(0, 3)],
        *[
            (cot_h.at[:, quarter_lanes(q)], s["cq"].at[quarter], dev)
            for q, dev in zip(quad_of, quads, strict=True)
        ],
    )
    s["brecv"][z] = s["bsend"][z]
    s["arecv"][z] = s["asend"][z]

    arrived(*pair)
    x_own = s["xv"].at[:, :, c][...].reshape(NX * NY * ROWS, FEATS)
    x_other = s["xp"][...].reshape(NX * NY * ROWS, FEATS)

    def project(j):
        cols = slice(j * QUARTER, (j + 1) * QUARTER)
        v = jnp.dot(x_own, s["wv"][:, cols], preferred_element_type=F32)
        v = v + jnp.dot(x_other, s["wp"][:, cols], preferred_element_type=F32)
        v = v.astype(BF16).reshape(NX, NY, ROWS, QUARTER)
        if j < 2:
            s["pa"][:, :, :, cols] = v
        else:
            cols = slice((j - 2) * QUARTER, (j - 1) * QUARTER)
            for xx in range(NX):
                s["pb"][:, xx, :, cols] = v[xx]

    for j in range(4):
        project(j)

    two = piece.at[pl.ds(0, 2)]

    def scatter_y(ds):
        return [(s["pb"].at[at_y(d)[0]], s["rb1"].at[d - 1], at_y(d)[1]) for d in ds]

    def scatter_y2(h):
        rows = pl.ds(2 * h, 2)
        yd, dev = at_y(2)
        return (s["pb"].at[yd, rows], s["rb1"].at[1, rows], dev)

    def scatter_x(ds):
        return [(s["pa"].at[at_xc(d, 0)[0]], s["ra1"].at[d - 1], at_xc(d, 0)[2]) for d in ds]

    rs1a = [push(two, *scatter_x((1, 3)))]
    rs1b = [push(two, *scatter_y((1, 3)))]
    mine0, mine1 = c0.at[:, y, c], c1.at[x, :, c]
    cot2a, cot2b, cot3 = [], [], []

    def to_partner(n, ref, where, ds):
        at = [ref.at[where(d)] for d in ds]
        cot3.append(push(piece.at[pl.ds(0, n)] if n > 1 else piece.at[0], *[(r, r, partner) for r in at]))

    def col(d):
        return (slice(None), lax.rem(y - d + NY, NY), c)

    def row(d):
        return (lax.rem(x - d + NX, NX), slice(None), c)

    arrived(*cot1)
    cot2b.append(push(two, *[(mine1, mine1, at_xc(d, 0)[2]) for d in (1, 3)]))
    cot3.append(push(two, (mine0, mine0, partner), (mine1, mine1, partner)))
    z_wait(0, s["bsend"])
    for k in range(NZ):
        s["bqf"][k * UP : (k + 1) * UP, :] = s["brecv"][k].astype(F32)
    up_own = s["bqf"][...].astype(BF16)
    s["bown"][quarter] = up_own
    last = (((1,), (1,)), ((), ()))
    arrived(quad_rows)
    locals_["cq"].wait()
    v = lax.dot_general(
        s["cq"][...].reshape(4 * ROWS, QUARTER), up_own, last, preferred_element_type=F32
    )
    v = jnp.concatenate([v[:COLS], v[COLS:]], axis=1)
    s["phs"][...] = v
    arrived(push(s["phr"], (s["phs"], s["phr"], partner)))
    lgp[x, y] = (v + s["phr"][...]).astype(BF16)
    mine = lgp.at[x, y]
    lgy = push(lgp.at[0, pl.ds(0, 3)], *[(mine, mine, at_y(d)[1]) for d in (1, 3, 2)])
    part = s["bown"].at[quarter]
    quad = push(s["bown"].at[pl.ds(0, 3)], *[(part, part, dev) for dev in quads])
    cot2a.append(push(two, *[(mine0, mine0, at_y(d)[1]) for d in (1, 3)]))
    cot2a.append(push(piece.at[0], (mine0, mine0, at_y(2)[1])))

    def gather_y(ref):
        r = ref.at[x, y, c]
        return push(s["ls"], *[(r, r, at_y(d)[1]) for d in (1, 3, 2)])

    def gather_x(ref):
        r = ref.at[x, :, c]
        return push(s["lr"], *[(r, r, at_xc(dx, dc)[2]) for dx, dc in rows7])

    arrived(lgy)
    mine = lgp.at[x]
    lgx = push(lgp.at[pl.ds(0, 3)], *[(mine, mine, at_xc(d, 0)[2]) for d in (1, 3, 2)])
    cot2b.append(push(piece.at[0], (mine1, mine1, at_xc(2, 0)[2])))

    def tok(b):
        return s["xv"][b // 2, 2 * (b % 2) : 2 * (b % 2) + 2].reshape(4 * ROWS, FEATS)

    def low_of(ref, b):
        return ref[b // 2, 2 * (b % 2) : 2 * (b % 2) + 2].reshape(4 * ROWS, RANKS)

    def down_of(b):
        return s["arecv"][:, b].reshape(FEATS, RANKS)

    first = (((0,), (0,)), ((), ()))
    arrived(lgx)
    narrow = lax.broadcasted_iota(I32, (COLS, RANKS), 1) < COLS
    for b in range(BLOCKS):
        key = lgp[b // 2, 2 * (b % 2)].astype(F32)
        val = lgp[b // 2, 2 * (b % 2) + 1].astype(F32)
        top = jnp.where(narrow, key, pltpu.roll(val, COLS, 1))
        bottom = jnp.where(narrow, pltpu.roll(key, COLS, 1), val)
        v = jnp.concatenate([top, bottom], axis=0).astype(BF16)
        s["lgm"][b] = v
        v = lax.dot_general(tok(b), v, first, preferred_element_type=F32)
        s["gaf"][pl.ds(b, FEATS, stride=BLOCKS), :] = v

    @pl.loop(0, NZ)
    def _(k):
        for r in range(DOWN):
            at = pl.ds(pl.multiple_of((k * DOWN + r) * BLOCKS, BLOCKS), BLOCKS)
            s["gasend"][k, :, r * RANKS : (r + 1) * RANKS] = s["gaf"][at, :].astype(BF16)

    z_send(2, s["gasend"], s["garecv"], 9, 15)
    s["garecv"][z] = s["gasend"][z]

    arrived(cot2a[0], cot2b[0])
    to_partner(2, c0, col, (1, 3))
    to_partner(2, c1, row, (1, 3))

    z_wait(1, s["asend"])

    for b in range(BLOCKS):
        v = jnp.dot(tok(b), down_of(b), preferred_element_type=F32)
        lp[b // 2, 2 * (b % 2) : 2 * (b % 2) + 2] = v.astype(BF16).reshape(2, 2, ROWS, RANKS)

    lowx = push(
        s["lr"],
        *[
            (lp.at[at_xc(dx, dc)[0], :, at_xc(dx, dc)[1]], s["lr"].at[n], at_xc(dx, dc)[2])
            for n, (dx, dc) in enumerate(rows7)
        ],
    )
    z_send(2, s["gasend"], s["garecv"], 0, 9)
    half = piece.at[0, pl.ds(0, 2)]
    rs1b.append(push(half, scatter_y2(0)))

    arrived(cot2b[1], cot2a[1])
    to_partner(1, c1, row, (2,))
    to_partner(1, c0, col, (2,))

    def total(own, ref, n):
        v = own.astype(F32)
        for k in range(n):
            v = v + ref[k].astype(F32)
        return v

    arrived(lowx)
    s["lq"][...] = total(lp.at[x, :, c][...], s["lr"], 7).astype(BF16)
    lowy = push(
        s["ls"], *[(s["lq"].at[at_y(d)[0]], s["ls"].at[d - 1], at_y(d)[1]) for d in (1, 3, 2)]
    )
    rs1a.append(push(piece.at[0], *scatter_x((2,))))

    arrived(*cot3)

    for xx in range(NX):
        rows = NY * 2 * ROWS
        v = lax.dot_general(
            c0[xx].reshape(rows, HALF), s["wv"][:, :HALF], last, preferred_element_type=F32
        )
        v = v + lax.dot_general(
            c1[xx].reshape(rows, HALF), s["wv"][:, HALF:], last, preferred_element_type=F32
        )
        low = [
            lax.dot_general(s["lgm"][2 * xx + k], down_of(2 * xx + k), last, preferred_element_type=F32)
            for k in range(2)
        ]
        ig_o[xx] = (v + jnp.concatenate(low, axis=0)).astype(BF16)


    arrived(lowy)
    la[x, y, c] = total(s["lq"][y], s["ls"], 3).astype(BF16)
    lay = gather_y(la)
    arrived(lay)
    last_low = gather_x(la)
    rs1b.append(push(half, scatter_y2(1)))
    arrived(*rs1a)
    for yy in range(NY):
        v = total(s["pa"][x, yy], s["ra1"].at[:, yy], 3)
        s["qa"][yy] = v.astype(BF16)
    rs2a = push(
        s["ra2"], *[(s["qa"].at[at_y(d)[0]], s["ra2"].at[d - 1], at_y(d)[1]) for d in (1, 3, 2)]
    )
    arrived(last_low)

    group = x * 8 + t
    chunk = pl.ds(pl.multiple_of(lax.rem(lax.div(group, 2), 8) * 128, 128), 128)
    values = lax.div(group, 16)

    def cot_cols(b):
        at = (b // 2, slice(2 * (b % 2), 2 * (b % 2) + 2), slice(None), slice(None), chunk)
        v = jnp.where(values == 0, c0[at].astype(F32), c1[at].astype(F32))
        return v.astype(BF16).reshape(4 * ROWS, 128)

    wide = lax.broadcasted_iota(I32, (COLS, 128), 1)

    def up_part(b):
        v = lax.dot_general(low_of(la, b), cot_cols(b), first, preferred_element_type=F32)
        v = jnp.where(values == 0, v[:COLS], v[COLS:])
        return v, pltpu.roll(v, COLS, 1)

    for b4 in range(4):
        lo, lo_r = up_part(b4)
        hi, hi_r = up_part(b4 + 4)
        left = jnp.where(c == 0, lo, lo_r)
        right = jnp.where(c == 0, hi_r, hi)
        v = jnp.where(wide < COLS, left, right)
        for k in range(NZ):
            s["gbf"][k, b4 * UP : (b4 + 1) * UP, :] = v[k * UP : (k + 1) * UP]
    s["gbsend"][...] = s["gbf"][...].astype(BF16)
    z_send(3, s["gbsend"], s["gbrecv"])
    s["gbrecv"][z] = s["gbsend"][z]

    arrived(*rs1b)
    for xx in range(NX):
        v = total(s["pb"][y, xx], s["rb1"].at[:, xx], 3)
        s["qb"][xx] = v.astype(BF16)
    rs2b = push(
        s["rb2"],
        *[(s["qb"].at[at_xc(d, 0)[0]], s["rb2"].at[d - 1], at_xc(d, 0)[2]) for d in (1, 3, 2)],
    )
    arrived(rs2a, rs2b, quad)
    low_rows = la[x, y, c]
    for j in range(4):
        cols = slice((j % 2) * QUARTER, (j % 2 + 1) * QUARTER)
        if j < 2:
            own, r1, r2 = s["pa"][x, y, :, cols], s["ra1"].at[:, y, :, cols], s["ra2"].at[:, :, cols]
        else:
            own, r1, r2 = s["pb"][y, x, :, cols], s["rb1"].at[:, x, :, cols], s["rb2"].at[:, :, cols]
        side = low_rows[:, :COLS] if j < 2 else low_rows[:, COLS:]
        v = total(total(own, r1, 3), r2, 3)
        v = v + jnp.dot(side, s["bown"][j], preferred_element_type=F32)
        kv_o[:, j * QUARTER : (j + 1) * QUARTER] = v.astype(BF16)

    ids = lax.broadcasted_iota(I32, (SLOTS, NZ * BLOCKS), 0)
    sel = jnp.where(ids == s["tga"][...], 1.0, 0.0).astype(BF16)
    z_wait(2, s["gasend"])
    for r in range(DOWN):
        lanes = slice(r * RANKS, (r + 1) * RANKS)
        data = s["garecv"][:, :, lanes].astype(F32).reshape(NZ * BLOCKS, RANKS).astype(BF16)
        v = jnp.dot(sel, data, preferred_element_type=F32)
        ga_o[pl.ds(r, SLOTS, stride=DOWN), :] = v

    z_wait(3, s["gbsend"])
    data = s["gbrecv"][...].reshape(NZ * DOWN, RANKS)
    ids = lax.broadcasted_iota(I32, (UP * SLOTS, NZ * DOWN), 0)
    sums = []
    for h in range(2):
        sel = jnp.where(ids == s["tgb"][h], 1.0, 0.0).astype(BF16)
        sums.append(jnp.dot(sel, data, preferred_element_type=F32))
    for i in range(UP):
        at = slice(i * SLOTS, (i + 1) * SLOTS)
        lo, hi = sums[0][at].T, sums[1][at].T
        gb_o[i] = lo[:COLS] + hi[COLS:]

    for i, like in enumerate(groups):
        until(like, s["ps"].at[i])
    for kind, name in enumerate(("bsend", "asend", "gasend", "gbsend")):
        until(s[name].at[pl.ds(0, NZ - 1)], s["zs"].at[kind])
    assert len(groups) == GROUPS, len(groups)

def body(tokens, weight, down, up, tenant_of_block, slot_of_tenant, cotangent):
    sc = scratches()
    anywhere = pl.BlockSpec(memory_space=pl.ANY)
    vmem = pl.BlockSpec(memory_space=pltpu.VMEM)
    results = (
        ((ROWS, WIDTH), BF16),
        ((NX, NY * 2 * ROWS, FEATS), BF16),
        ((SLOTS * DOWN, RANKS), F32),
        ((UP, COLS, SLOTS), F32),
    )
    kv, ig, ga, gb = pl.pallas_call(
        functools.partial(kern, tuple(sc)),
        out_shape=tuple(pltpu.VMEM(shape, kind) for shape, kind in results),
        in_specs=[anywhere] * 7,
        out_specs=(vmem,) * 4,
        scratch_shapes=list(sc.values()),
        compiler_params=pltpu.CompilerParams(
            collective_id=0, has_side_effects=True, vmem_limit_bytes=60 * 1024 * 1024
        ),
    )(
        tenant_of_block,
        slot_of_tenant,
        tokens.reshape(NX, NY, 2, ROWS, FEATS),
        weight,
        down,
        up,
        cotangent,
    )
    return (
        kv,
        ig.reshape(NX * NY * 2 * ROWS, FEATS),
        ga.reshape(SLOTS, DOWN, RANKS),
        gb.transpose(2, 0, 1),
    )


def solution(mesh):
    placed = (
        P("dp", ("pipe", "tensor")),
        P(("pipe", "tensor"), None),
        P(None, ("pipe", "tensor", "dp"), None),
        P(None, "dp", None),
        P(),
        P(),
        P(("dp", "pipe", "tensor"), None),
    )
    return jax.shard_map(
        body,
        mesh=mesh,
        in_specs=placed,
        out_specs=(
            P(("dp", "pipe", "tensor"), None),
            P("dp", ("pipe", "tensor")),
            P(None, ("pipe", "tensor", "dp"), None),
            P(None, "dp", ("pipe", "tensor")),
        ),
        check_vma=False,
    )
```

time: 92.8 us -> 74.4 us (0.80)
  Pallas kernels: 86.9 us -> 70.7 us
  local copies, waits for them, and re-layouts: 5.06 us -> 2.98 us
    pallas_call x1, Pallas kernels: 86.9 us -> 70.7 us  [body(): pl.pallas_call(functools.partial(kern, tuple(sc)), out_shape=tuple((pltpu...]
    unnamed x8 -> x4, local copies, waits for them, and re-layouts: 5.06 us -> 2.98 us
where the time goes in v2:
time: 74.4 us; the launch traced here: 74.3 us
  Pallas kernels  70.7 us (95%)
  local copies, waits for them, and re-layouts  2.98 us (4%)
    pallas_call x1, Pallas kernels, body(): pl.pallas_call(functools.partial(kern, tuple(sc)), out_shape=tuple((pltpu...  70.7 us
    unnamed x4, local copies, waits for them, and re-layouts  2.98 us

profile of v2, /device:TPU:1, one launch (start us, length us, event | category | flops | bytes accessed | tf_op | source)
XLA Modules:
  0.0 74.3 jit_solution(5048542272649626405)
XLA Ops:
  0.6 70.7 %shard_map.102 = (bf16[32,2048]{1,0:T(8,128)(2,1)S(1)}, bf16[4,256,256]{2,1,0:T(8,128)(2,1)S(1)}, f32[1536,128]{1,0:T(8,128)S(1)}, f32[4,64,96]{2,1,0:T(8,128)S(1)}) custom-call(s32[128]{0:T(128)} %ten_h.1, s32[96]{0:T(128)} %slot_h.1, bf16[4,4,2,32,256]{4,3,2,1,0:T(8,128)(2,1)} %bitcast.7, bf16[256,2048]{1,0:T(8,128)(2,1)} %w_h.1, ...), custom_call_target="tpu_custom_call" | custom-call | tf_op jit(solution)/shard_map/pallas_call | solution.py:508
  71.3 0.7 copy.15
  72.0 0.8 %copy.16 = bf16[1024,256]{1,0:T(8,128)(2,1)} copy(bf16[1024,256]{1,0:T(8,128)(2,1)S(1)} %bitcast.5) | data formatting | bytes 1048576
  72.7 0.7 copy.18
  73.4 0.9 %copy.17 = f32[96,16,128]{2,1,0:T(8,128)} copy(f32[96,16,128]{2,1,0:T(8,128)S(1)} %bitcast.4) | data formatting | bytes 1572864

commit v3 on v2

--- a/solution.py
+++ b/solution.py
@@ -14,7 +14,7 @@
 BLOCKS = 8
 ROWS, FEATS, WIDTH, HALF, QUARTER = 32, 256, 2048, 1024, 512
 COLS = 64
-GROUPS = 29
+GROUPS = 28
 
 
 def scratches():
@@ -257,11 +257,6 @@
     def scatter_y(ds):
         return [(s["pb"].at[at_y(d)[0]], s["rb1"].at[d - 1], at_y(d)[1]) for d in ds]
 
-    def scatter_y2(h):
-        rows = pl.ds(2 * h, 2)
-        yd, dev = at_y(2)
-        return (s["pb"].at[yd, rows], s["rb1"].at[1, rows], dev)
-
     def scatter_x(ds):
         return [(s["pa"].at[at_xc(d, 0)[0]], s["ra1"].at[d - 1], at_xc(d, 0)[2]) for d in ds]
 
@@ -300,10 +295,6 @@
     lgp[x, y] = (v + s["phr"][...]).astype(BF16)
     mine = lgp.at[x, y]
     lgy = push(lgp.at[0, pl.ds(0, 3)], *[(mine, mine, at_y(d)[1]) for d in (1, 3, 2)])
-    part = s["bown"].at[quarter]
-    quad = push(s["bown"].at[pl.ds(0, 3)], *[(part, part, dev) for dev in quads])
-    cot2a.append(push(two, *[(mine0, mine0, at_y(d)[1]) for d in (1, 3)]))
-    cot2a.append(push(piece.at[0], (mine0, mine0, at_y(2)[1])))
 
     def gather_y(ref):
         r = ref.at[x, y, c]
@@ -313,10 +304,14 @@
         r = ref.at[x, :, c]
         return push(s["lr"], *[(r, r, at_xc(dx, dc)[2]) for dx, dc in rows7])
 
+    cot2a.append(push(two, *[(mine0, mine0, at_y(d)[1]) for d in (1, 3)]))
+    cot2a.append(push(piece.at[0], (mine0, mine0, at_y(2)[1])))
     arrived(lgy)
     mine = lgp.at[x]
     lgx = push(lgp.at[pl.ds(0, 3)], *[(mine, mine, at_xc(d, 0)[2]) for d in (1, 3, 2)])
     cot2b.append(push(piece.at[0], (mine1, mine1, at_xc(2, 0)[2])))
+    part = s["bown"].at[quarter]
+    quad = push(s["bown"].at[pl.ds(0, 3)], *[(part, part, dev) for dev in quads])
 
     def tok(b):
         return s["xv"][b // 2, 2 * (b % 2) : 2 * (b % 2) + 2].reshape(4 * ROWS, FEATS)
@@ -346,7 +341,7 @@
             at = pl.ds(pl.multiple_of((k * DOWN + r) * BLOCKS, BLOCKS), BLOCKS)
             s["gasend"][k, :, r * RANKS : (r + 1) * RANKS] = s["gaf"][at, :].astype(BF16)
 
-    z_send(2, s["gasend"], s["garecv"], 9, 15)
+    z_send(2, s["gasend"], s["garecv"], 9, 13)
     s["garecv"][z] = s["gasend"][z]
 
     arrived(cot2a[0], cot2b[0])
@@ -367,8 +362,7 @@
         ],
     )
     z_send(2, s["gasend"], s["garecv"], 0, 9)
-    half = piece.at[0, pl.ds(0, 2)]
-    rs1b.append(push(half, scatter_y2(0)))
+    rs1b.append(push(piece.at[0], *scatter_y((2,))))
 
     arrived(cot2b[1], cot2a[1])
     to_partner(1, c1, row, (2,))
@@ -409,7 +403,6 @@
     lay = gather_y(la)
     arrived(lay)
     last_low = gather_x(la)
-    rs1b.append(push(half, scatter_y2(1)))
     arrived(*rs1a)
     for yy in range(NY):
         v = total(s["pa"][x, yy], s["ra1"].at[:, yy], 3)
@@ -445,6 +438,7 @@
             s["gbf"][k, b4 * UP : (b4 + 1) * UP, :] = v[k * UP : (k + 1) * UP]
     s["gbsend"][...] = s["gbf"][...].astype(BF16)
     z_send(3, s["gbsend"], s["gbrecv"])
+    z_send(2, s["gasend"], s["garecv"], 13, 15)
     s["gbrecv"][z] = s["gbsend"][z]
 
     arrived(*rs1b)
@@ -455,6 +449,16 @@
         s["rb2"],
         *[(s["qb"].at[at_xc(d, 0)[0]], s["rb2"].at[d - 1], at_xc(d, 0)[2]) for d in (1, 3, 2)],
     )
+
+    ids = lax.broadcasted_iota(I32, (SLOTS, NZ * BLOCKS), 0)
+    sel = jnp.where(ids == s["tga"][...], 1.0, 0.0).astype(BF16)
+    z_wait(2, s["gasend"])
+    for r in range(DOWN):
+        lanes = slice(r * RANKS, (r + 1) * RANKS)
+        data = s["garecv"][:, :, lanes].astype(F32).reshape(NZ * BLOCKS, RANKS).astype(BF16)
+        v = jnp.dot(sel, data, preferred_element_type=F32)
+        ga_o[pl.ds(r, SLOTS, stride=DOWN), :] = v
+
     arrived(rs2a, rs2b, quad)
     low_rows = la[x, y, c]
     for j in range(4):
@@ -468,15 +472,6 @@
         v = v + jnp.dot(side, s["bown"][j], preferred_element_type=F32)
         kv_o[:, j * QUARTER : (j + 1) * QUARTER] = v.astype(BF16)
 
-    ids = lax.broadcasted_iota(I32, (SLOTS, NZ * BLOCKS), 0)
-    sel = jnp.where(ids == s["tga"][...], 1.0, 0.0).astype(BF16)
-    z_wait(2, s["gasend"])
-    for r in range(DOWN):
-        lanes = slice(r * RANKS, (r + 1) * RANKS)
-        data = s["garecv"][:, :, lanes].astype(F32).reshape(NZ * BLOCKS, RANKS).astype(BF16)
-        v = jnp.dot(sel, data, preferred_element_type=F32)
-        ga_o[pl.ds(r, SLOTS, stride=DOWN), :] = v
-
     z_wait(3, s["gbsend"])
     data = s["gbrecv"][...].reshape(NZ * DOWN, RANKS)
     ids = lax.broadcasted_iota(I32, (UP * SLOTS, NZ * DOWN), 0)
@@ -494,6 +489,15 @@
     for kind, name in enumerate(("bsend", "asend", "gasend", "gbsend")):
         until(s[name].at[pl.ds(0, NZ - 1)], s["zs"].at[kind])
     assert len(groups) == GROUPS, len(groups)
+
+def write_out(kv, ig, ga, gb, kv_o, ig_o, ga_o, gb_o, sem):
+    pairs = ((ga, ga_o), (ig, ig_o), (kv, kv_o), (gb, gb_o))
+    copies = [pltpu.make_async_copy(v, o, sem.at[i]) for i, (v, o) in enumerate(pairs)]
+    for cp in copies:
+        cp.start()
+    for cp in copies:
+        cp.wait()
+
 
 def body(tokens, weight, down, up, tenant_of_block, slot_of_tenant, cotangent):
     sc = scratches()
@@ -523,6 +527,14 @@
         up,
         cotangent,
     )
+    near = [pltpu.with_memory_space_constraint(v, pltpu.VMEM) for v in (kv, ig, ga, gb)]
+    kv, ig, ga, gb = pl.pallas_call(
+        write_out,
+        out_shape=tuple(jax.ShapeDtypeStruct(shape, kind) for shape, kind in results),
+        in_specs=[vmem] * 4,
+        out_specs=(anywhere,) * 4,
+        scratch_shapes=[pltpu.SemaphoreType.DMA((4,))],
+    )(*near)
     return (
         kv,
         ig.reshape(NX * NY * 2 * ROWS, FEATS),

time: 74.4 us -> 72.4 us (0.973)
  local copies, waits for them, and re-layouts: 2.98 us -> 0 us
  Pallas kernels: 70.7 us -> 71.5 us
    unnamed x4 -> x0, local copies, waits for them, and re-layouts: 2.98 us -> none
    pallas_call x0 -> x1, Pallas kernels: none -> 1.17 us  [body(): pl.pallas_call(write_out, out_shape=tuple((jax.ShapeDtypeStruct(shape, ki...]
where the time goes in v3:
time: 72.4 us; the launch traced here: 72.1 us
  Pallas kernels  71.5 us (99%)
    pallas_call x1, Pallas kernels, body(): pl.pallas_call(functools.partial(kern, tuple(sc)), out_shape=tuple((pltpu...  70.3 us

profile of v3, /device:TPU:1, one launch (start us, length us, event | category | flops | bytes accessed | tf_op | source)
XLA Modules:
  0.0 72.1 jit_solution(11803527503571927491)
XLA Ops:
  0.6 70.3 %shard_map.102 = (bf16[32,2048]{1,0:T(8,128)(2,1)S(1)}, bf16[4,256,256]{2,1,0:T(8,128)(2,1)S(1)}, f32[1536,128]{1,0:T(8,128)S(1)}, f32[4,64,96]{2,1,0:T(8,128)S(1)}) custom-call(s32[128]{0:T(128)} %ten_h.1, s32[96]{0:T(128)} %slot_h.1, bf16[4,4,2,32,256]{4,3,2,1,0:T(8,128)(2,1)} %bitcast.4, bf16[256,2048]{1,0:T(8,128)(2,1)} %w_h.1, ...), custom_call_target="tpu_custom_call" | custom-call | tf_op jit(solution)/shard_map/pallas_call | solution.py:512
  71.0 1.2 %shard_map.103 = (bf16[32,2048]{1,0:T(8,128)(2,1)}, bf16[4,256,256]{2,1,0:T(8,128)(2,1)}, f32[1536,128]{1,0:T(8,128)}, f32[4,64,96]{2,1,0:T(8,128)}) custom-call(bf16[32,2048]{1,0:T(8,128)(2,1)S(1)} %get-tuple-element.12.kv, bf16[4,256,256]{2,1,0:T(8,128)(2,1)S(1)} %get-tuple-element.13.ig, f32[1536,128]{1,0:T(8,128)S(1)} %get-tuple-element.14.ga, ...), custom_call_target="tpu_custom_call" | custom-call | tf_op jit(solution)/shard_map/pallas_call | solution.py:531

commit v4 on v3

--- a/solution.py
+++ b/solution.py
@@ -305,11 +305,10 @@
         return push(s["lr"], *[(r, r, at_xc(dx, dc)[2]) for dx, dc in rows7])
 
     cot2a.append(push(two, *[(mine0, mine0, at_y(d)[1]) for d in (1, 3)]))
-    cot2a.append(push(piece.at[0], (mine0, mine0, at_y(2)[1])))
+    rs1b.append(push(piece.at[0], *scatter_y((2,))))
     arrived(lgy)
     mine = lgp.at[x]
     lgx = push(lgp.at[pl.ds(0, 3)], *[(mine, mine, at_xc(d, 0)[2]) for d in (1, 3, 2)])
-    cot2b.append(push(piece.at[0], (mine1, mine1, at_xc(2, 0)[2])))
     part = s["bown"].at[quarter]
     quad = push(s["bown"].at[pl.ds(0, 3)], *[(part, part, dev) for dev in quads])
 
@@ -345,6 +344,11 @@
     s["garecv"][z] = s["gasend"][z]
 
     arrived(cot2a[0], cot2b[0])
+    lo, hi = pl.ds(0, 2), pl.ds(2, 2)
+    up0, down0 = c0.at[lo, col(1)[1], c], c0.at[hi, col(3)[1], c]
+    cot2a.append(push(piece.at[0], (up0, up0, at_y(1)[1]), (down0, down0, at_y(3)[1])))
+    up1, down1 = c1.at[row(1)[0], lo, c], c1.at[row(3)[0], hi, c]
+    cot2b.append(push(piece.at[0], (up1, up1, at_xc(1, 0)[2]), (down1, down1, at_xc(3, 0)[2])))
     to_partner(2, c0, col, (1, 3))
     to_partner(2, c1, row, (1, 3))
 
@@ -362,7 +366,6 @@
         ],
     )
     z_send(2, s["gasend"], s["garecv"], 0, 9)
-    rs1b.append(push(piece.at[0], *scatter_y((2,))))
 
     arrived(cot2b[1], cot2a[1])
     to_partner(1, c1, row, (2,))

time: 72.4 us -> 72.2 us (level)
  no operation moved by 1% of the time
where the time goes in v4:
time: 72.2 us; the launch traced here: 72.1 us
  Pallas kernels  71.5 us (99%)
    pallas_call x1, Pallas kernels, body(): pl.pallas_call(functools.partial(kern, tuple(sc)), out_shape=tuple((pltpu...  70.3 us

profile of v4, /device:TPU:1, one launch (start us, length us, event | category | flops | bytes accessed | tf_op | source)
XLA Modules:
  0.0 72.1 jit_solution(10433466054798106438)
XLA Ops:
  0.6 70.3 %shard_map.102 = (bf16[32,2048]{1,0:T(8,128)(2,1)S(1)}, bf16[4,256,256]{2,1,0:T(8,128)(2,1)S(1)}, f32[1536,128]{1,0:T(8,128)S(1)}, f32[4,64,96]{2,1,0:T(8,128)S(1)}) custom-call(s32[128]{0:T(128)} %ten_h.1, s32[96]{0:T(128)} %slot_h.1, bf16[4,4,2,32,256]{4,3,2,1,0:T(8,128)(2,1)} %bitcast.4, bf16[256,2048]{1,0:T(8,128)(2,1)} %w_h.1, ...), custom_call_target="tpu_custom_call" | custom-call | tf_op jit(solution)/shard_map/pallas_call | solution.py:515
  70.9 1.2 %shard_map.103 = (bf16[32,2048]{1,0:T(8,128)(2,1)}, bf16[4,256,256]{2,1,0:T(8,128)(2,1)}, f32[1536,128]{1,0:T(8,128)}, f32[4,64,96]{2,1,0:T(8,128)}) custom-call(bf16[32,2048]{1,0:T(8,128)(2,1)S(1)} %get-tuple-element.12.kv, bf16[4,256,256]{2,1,0:T(8,128)(2,1)S(1)} %get-tuple-element.13.ig, f32[1536,128]{1,0:T(8,128)S(1)} %get-tuple-element.14.ga, ...), custom_call_target="tpu_custom_call" | custom-call | tf_op jit(solution)/shard_map/pallas_call | solution.py:534
